TPU v7x, 32 devices: a whole 2x2x4 slice. The times are simulated.
32 devices in a mesh: win: 2 (over y), vel: 8 (over z, x), sp: 2 (over core).
Axes of the slice: x: 2, y: 2, z: 4, core: 2. Of those that a mesh axis runs over, the one named last changes fastest.
Arguments:
- f_start: float32 [2, 1536, 64, 128], P('win', 'vel', 'sp'), may hold values from 0 to 15, as said below
- relax_rate: float32 [64, 128], P('sp'), may hold values from 0.1 to 10
Outputs:
- corrected: float32 [2, 4, 64, 128], P('win', None, 'sp')
- lifted: float32 [2, 1536, 64, 128], P('win', 'vel', 'sp')
Inputs may be any that keep to these rules, and one draw needn't show every extreme that they name: `f_start`: no entry is negative.
All inputs are finite; a program needn't handle non-finite values.
Results may differ from a plain program's by a relative error of at most 0.00021.
Values sent between devices are 32-bit elements; how exact they have to be, the bound alone decides.
A program may use at most 64 MiB of HBM per device.

v0:
```python
import math

import jax
import jax.numpy as jnp
from jax import lax
from jax.sharding import PartitionSpec as P

NVX = 48
NVY = 32


vel_max = 6.0
fine_ratio = 0.075
coarse_ratio = 0.15
density_floor = 0.3
thermal_lower_bound = 0.3


def with_halo(block, sides, width):
    for axis, dim in sides:
        count = lax.axis_size(axis)
        forward = [(i, i + 1) for i in range(count - 1)]
        forward.append((count - 1, 0))
        backward = [(target, source) for source, target in forward]
        low = lax.ppermute(
            lax.slice_in_dim(block, block.shape[dim] - width, None, axis=dim), axis, forward
        )
        high = lax.ppermute(lax.slice_in_dim(block, 0, width, axis=dim), axis, backward)
        block = jnp.concatenate([low, block, high], axis=dim)
    return block


def shifted(value, axis, steps):
    count = lax.axis_size(axis)
    leading, last = (max(0, -steps), min(count, count - steps))
    return lax.ppermute(value, axis, [(source, source + steps) for source in range(leading, last)])


def velocity_table(first, count):
    index = first + jnp.arange(count, dtype=jnp.int32)
    vel_x = -vel_max + ((index // NVY).astype(jnp.float32) + 0.5) * (2.0 * vel_max / NVX)
    vel_y = -vel_max + ((index % NVY).astype(jnp.float32) + 0.5) * (2.0 * vel_max / NVY)
    return (vel_x, vel_y)


def moment_table(vel_x, vel_y):
    weight_unit = 2.0 * vel_max / NVX * (2.0 * vel_max / NVY) / (2.0 * math.pi)
    return (
        jnp.stack([jnp.ones_like(vel_x), vel_x, vel_y, 0.5 * (vel_x * vel_x + vel_y * vel_y)])
        * weight_unit
    )


def moments(field, table):
    flat = field.reshape(field.shape[0], -1)
    out = jnp.dot(table, flat, precision=lax.Precision.HIGHEST, preferred_element_type=jnp.float32)
    return out.reshape(4, field.shape[1], field.shape[2])


def physical_variables(distribution_array):
    mass_per_volume = jnp.maximum(distribution_array[0], density_floor)
    horizontal_flow = distribution_array[1] / mass_per_volume
    upward_flow = distribution_array[2] / mass_per_volume
    inner_volumes = (
        distribution_array[3]
        - 0.5 * (distribution_array[1] * horizontal_flow + distribution_array[2] * upward_flow)
    ) / mass_per_volume
    pointwise_thermal_level = jnp.maximum(inner_volumes, thermal_lower_bound)
    return (mass_per_volume, horizontal_flow, upward_flow, pointwise_thermal_level)


def equilibrium_density(distribution_array, vel_x, vel_y):
    mass_per_volume, horizontal_flow, upward_flow, pointwise_thermal_level = physical_variables(
        distribution_array
    )
    horizontal_gradient = vel_x[:, None, None] - horizontal_flow[None]
    upward_gradient = vel_y[:, None, None] - upward_flow[None]
    return (mass_per_volume / pointwise_thermal_level)[None] * jnp.exp(
        -(horizontal_gradient * horizontal_gradient + upward_gradient * upward_gradient)
        / (2.0 * pointwise_thermal_level[None])
    )


def transport(field, left, right, vel_x, vel_y):
    coef_x = (vel_x * fine_ratio)[:, None, None]
    coef_y = (vel_y * fine_ratio)[:, None, None]
    below = jnp.roll(field, 1, axis=2)
    above = jnp.roll(field, -1, axis=2)
    out = (
        field
        - jnp.maximum(coef_x, 0.0) * (field - left)
        - jnp.minimum(coef_x, 0.0) * (right - field)
    )
    return (
        out
        - jnp.maximum(coef_y, 0.0) * (field - below)
        - jnp.minimum(coef_y, 0.0) * (above - field)
    )


def euler_update(padded_array):
    mass_per_volume, horizontal_flow, upward_flow, pointwise_thermal_level = physical_variables(
        padded_array
    )
    normal_stress = mass_per_volume * pointwise_thermal_level
    acoustic_wave_rate = jnp.sqrt(2.0 * pointwise_thermal_level)
    flux_x = jnp.stack(
        [
            padded_array[1],
            padded_array[1] * horizontal_flow + normal_stress,
            padded_array[2] * horizontal_flow,
            (padded_array[3] + normal_stress) * horizontal_flow,
        ]
    )
    flux_y = jnp.stack(
        [
            padded_array[2],
            padded_array[1] * upward_flow,
            padded_array[2] * upward_flow + normal_stress,
            (padded_array[3] + normal_stress) * upward_flow,
        ]
    )
    reach_x = jnp.abs(horizontal_flow) + acoustic_wave_rate
    reach_y = jnp.abs(upward_flow) + acoustic_wave_rate
    face_x = 0.5 * (flux_x[:, :-1, 1:-1] + flux_x[:, 1:, 1:-1]) - 0.5 * jnp.maximum(
        reach_x[:-1, 1:-1], reach_x[1:, 1:-1]
    )[None] * (padded_array[:, 1:, 1:-1] - padded_array[:, :-1, 1:-1])
    face_y = 0.5 * (flux_y[:, 1:-1, :-1] + flux_y[:, 1:-1, 1:]) - 0.5 * jnp.maximum(
        reach_y[1:-1, :-1], reach_y[1:-1, 1:]
    )[None] * (padded_array[:, 1:-1, 1:] - padded_array[:, 1:-1, :-1])
    return padded_array[:, 1:-1, 1:-1] - coarse_ratio * (
        face_x[:, 1:] - face_x[:, :-1] + (face_y[:, :, 1:] - face_y[:, :, :-1])
    )


def coarse_step(distribution_array):
    padded_array = with_halo(distribution_array, (("sp", 1),), 1)
    padded_array = jnp.concatenate(
        [padded_array[:, :, -1:], padded_array, padded_array[:, :, :1]], axis=2
    )
    return euler_update(padded_array)


def advance(current, vel_x, vel_y):
    padded_array = with_halo(current, (("sp", 1),), 1)
    return transport(current, padded_array[:, :-2], padded_array[:, 2:], vel_x, vel_y)


def per_device(f_start, relax_rate):
    field = f_start[0]
    count = field.shape[0]
    vel_x, vel_y = velocity_table(lax.axis_index("vel") * count, count)
    table = moment_table(vel_x, vel_y)
    rates = relax_rate[None]
    local_start = moments(field, table)
    start = lax.psum(local_start, "vel")
    current = field
    for step in range(2):
        star = advance(current, vel_x, vel_y)
        distribution_array = lax.psum(moments(star, table), "vel")
        current = (star + rates * equilibrium_density(distribution_array, vel_x, vel_y)) / (
            1.0 + rates
        )
    delta = distribution_array - coarse_step(start)
    windows = lax.axis_size("win")
    position = lax.axis_index("win")
    carried = start
    for turn in range(windows):
        result = coarse_step(carried) + delta
        if turn + 1 < windows:
            passed = shifted(result, "win", 1)
            carried = jnp.where(position == 0, start, passed)
    lifted = (
        current
        + equilibrium_density(result, vel_x, vel_y)
        - equilibrium_density(distribution_array, vel_x, vel_y)
    )
    return (result[None], lifted[None])


def solution(mesh):
    return jax.shard_map(
        per_device,
        mesh=mesh,
        in_specs=(P("win", "vel", "sp", None), P("sp", None)),
        out_specs=(P("win", None, "sp", None), P("win", "vel", "sp", None)),
        check_vma=False,
    )
```

profile of v0, /device:TPU:0, one launch (start us, length us, event | category | flops | bytes accessed | tf_op | source)
XLA Modules:
  0.0 217.6 jit_solution(6024811357756668443)
XLA Ops:
  7.2 2.2 fusion.107
  9.9 6.6 %fusion.105 = (f32[192,32,127]{2,1,0:T(8,128)}, f32[192,32,127]{2,1,0:T(8,128)}) fusion(f32[192,32,128]{2,1,0:T(8,128)} %bitcast.194), kind=kLoop, calls=%fused_computation.217 | loop fusion | bytes 12484608 | tf_op jit(solution)/shard_map/jit(_roll_static)/slice | solution.py:88
  16.5 3.9 %fusion.106 = (f32[192,32,1]{2,1,0:T(8,128)}, f32[192,32,1]{2,1,0:T(8,128)}) fusion(f32[192,32,128]{2,1,0:T(8,128)S(1)} %bitcast.195), kind=kLoop, calls=%fused_computation.218 | loop fusion | bytes 98304 | tf_op jit(solution)/shard_map/jit(_roll_static)/slice | solution.py:88
  20.4 3.9 %fusion.6 = f32[4,32,128]{2,0,1:T(4,128)} fusion(f32[1,192]{1,0:T(1,128)S(1)} %get-tuple-element.77, f32[1,192]{1,0:T(1,128)S(1)} %get-tuple-element.76, f32[1,192]{1,0:T(1,128)S(1)} %multiply_add_fusion.4, f32[4]{0:T(128)S(1)} %pad.72.clone, f32[24,8,32,128]{3,2,1,0:T(8,128)S(1)} %bitcast.196), kind=kOutput, calls=%fused_computation.9 | convolution fusion | flops 37751808 | bytes 3213584 | tf_op jit(solution)/shard_map/dot_general | solution.py:56
  24.4 6.2 %fusion.21 = f32[192,32,128]{2,1,0:T(8,128)S(1)} fusion(f32[192,32,128]{2,1,0:T(8,128)S(1)} %bitcast.197, f32[192,1,128]{2,1,0:T(1,128)S(1)} %collective-permute-done.3, f32[192,1,128]{2,1,0:T(1,128)S(1)} %collective-permute-done.2, f32[192,32,127]{2,1,0:T(8,128)} %get-tuple-element.42, f32[192,32,1]{2,1,0:T(8,128)} %get-tuple-element.44, ...), kind=kLoop, calls=%fused_computation.27 | loop fusion | flops 12582912 | bytes 12782592 | tf_op jit(solution)/shard_map/sub | solution.py:95
  30.7 1.7 copy-done.1
  32.3 3.9 %fusion.3 = f32[4,32,128]{2,0,1:T(4,128)} fusion(f32[1,192]{1,0:T(1,128)S(1)} %get-tuple-element.77, f32[1,192]{1,0:T(1,128)S(1)} %get-tuple-element.76, f32[1,192]{1,0:T(1,128)S(1)} %multiply_add_fusion.4, f32[4]{0:T(128)S(1)} %pad.72.clone, f32[24,8,32,128]{3,2,1,0:T(8,128)S(1)} %bitcast.199), kind=kOutput, calls=%fused_computation.6 | convolution fusion | flops 37751808 | bytes 3213584 | tf_op jit(solution)/shard_map/dot_general | solution.py:56
  36.5 71.9 %all-reduce.4.cloned.1.call-done = f32[4,32,128]{2,0,1:T(4,128)} async-done(((f32[4,32,128]{2,0,1:T(4,128)}), f32[4,32,128]{2,0,1:T(4,128)}) %all-reduce.4.cloned.1.call-update) | async-done | bytes 65552 | tf_op jit(solution)/shard_map/psum | solution.py:160
  108.4 1.1 fusion.90
  109.5 2.9 %add_divide_fusion = f32[192,32,128]{2,1,0:T(8,128)S(1)} fusion(f32[192,32,128]{2,1,0:T(8,128)} %copy-done.1, f32[32,128]{1,0:T(8,128)S(1)} %broadcast_add_fusion, f32[32,128]{1,0:T(8,128)S(1)} %bitcast.210, f32[32,128]{1,0:T(8,128)S(1)} %bitcast.219, f32[192]{0:T(256)S(1)} %get-tuple-element.78, f32[32,128]{1,0:T(8,128)S(1)} %bitcast.218, ...), kind=kLoop, calls=%fused_computation.41 | loop fusion | flops 8650752 | bytes 6391296 | tf_op jit(solution)/shard_map/div | solution.py:161
  112.4 1.1 fusion.102
  113.7 0.5 collective-permute-start.5
  114.2 1.1 fusion.103
  115.4 3.9 %fusion.13 = f32[192,32,128]{2,1,0:T(8,128)S(1)} fusion(f32[192,32,128]{2,1,0:T(8,128)S(1)} %add_divide_fusion, f32[192,1,128]{2,1,0:T(1,128)S(1)} %collective-permute-done.5, f32[192,1,128]{2,1,0:T(1,128)S(1)} %collective-permute-done.4, f32[192,32,127]{2,1,0:T(8,128)S(1)} %get-tuple-element.36, f32[192,32,1]{2,1,0:T(8,128)S(1)} %get-tuple-element.38, ...), kind=kLoop, calls=%fused_computation.17 | loop fusion | flops 12582912 | bytes 12782592 | tf_op jit(solution)/shard_map/sub | solution.py:95
  119.3 3.9 %fusion = f32[4,32,128]{2,0,1:T(4,128)} fusion(f32[1,192]{1,0:T(1,128)S(1)} %get-tuple-element.77, f32[1,192]{1,0:T(1,128)S(1)} %get-tuple-element.76, f32[1,192]{1,0:T(1,128)S(1)} %multiply_add_fusion.4, f32[4]{0:T(128)S(1)} %pad.72.clone, f32[24,8,32,128]{3,2,1,0:T(8,128)S(1)} %bitcast.198), kind=kOutput, calls=%fused_computation.3 | convolution fusion | flops 37751808 | bytes 3213584 | tf_op jit(solution)/shard_map/dot_general | solution.py:56
  123.2 70.8 %all-reduce.6.cloned.1.call-done = (f32[4,32,128]{2,0,1:T(4,128)}, f32[4,32,128]{2,0,1:T(4,128)}) async-done(((f32[4,32,128]{2,0,1:T(4,128)}, f32[4,32,128]{2,0,1:T(4,128)}), (f32[4,32,128]{2,0,1:T(4,128)}, f32[4,32,128]{2,0,1:T(4,128)})) %all-reduce.6.cloned.1.call-update) | async-done | bytes 131088 | tf_op jit(solution)/shard_map/psum | solution.py:160
  194.0 0.7 fusion.113
  194.8 0.5 collective-permute-start.1
  195.3 0.8 copy.29
  197.5 3.4 %collective-permute-start.6 = (f32[4,32,128]{2,0,1:T(4,128)S(1)}, f32[4,32,128]{2,0,1:T(4,128)S(1)}, u32[]{:S(2)}, u32[]{:S(2)}) collective-permute-start(f32[4,32,128]{2,0,1:T(4,128)S(1)} %get-tuple-element.23), channel_id=1, source_target_pairs={{0,16},{1,17},{2,18},{3,19},{4,20},{5,21},{6,22},{7,23},{8,24},{9,... | collective-permute-start | bytes 196616 | tf_op jit(solution)/shard_map/ppermute | solution.py:36
  200.9 1.8 collective-permute-done.6
  203.4 0.6 collective-permute-done.7
  206.2 0.6 copy.52
  206.9 3.8 %subtract_bitcast_fusion = f32[1,192,32,128]{3,2,1,0:T(8,128)} fusion(f32[192,32,128]{2,1,0:T(8,128)S(1)} %fusion.13, f32[32,128]{1,0:T(8,128)S(1)} %bitcast.209, f32[32,128]{1,0:T(8,128)S(1)} %bitcast.216, f32[32,128]{1,0:T(8,128)S(1)} %bitcast.215, f32[32,128]{1,0:T(8,128)S(1)} %bitcast.214, f32[32,128]{1,0:T(8,128)S(1)} %bitcast.208, ...), kind=kLoop, calls=%fused_computation.40 | loop fusion | flops 16515072 | bytes 6456832 | tf_op jit(solution)/shard_map/broadcast_in_dim | solution.py:178
  (78 shorter events, 5.2 us)
Async XLA Ops:
  7.2 101.2 %all-reduce.4.cloned.1.call-start = ((), (), s32[]{:S(2)}) async-start(), calls=%async_computation | async-start | bytes 131072 | tf_op jit(solution)/shard_map/psum | solution.py:160
  9.4 15.0 %collective-permute-start.2 = (f32[192,1,128]{2,1,0:T(1,128)}, f32[192,1,128]{2,1,0:T(1,128)S(1)}, u32[]{:S(2)}, u32[]{:S(2)}) collective-permute-start(f32[192,1,128]{2,1,0:T(1,128)} %get-tuple-element.45), channel_id=1, source_target_pairs={{0,1},{1,0},{2,3},{3,2},{4,5},{5,4},{6,7},{7,6},{8,9},{9,8},{10,11... | collective-permute-start | bytes 294920 | tf_op jit(solution)/shard_map/ppermute | solution.py:25
  9.9 14.5 %collective-permute-start.3 = (f32[192,1,128]{2,1,0:T(1,128)S(1)}, f32[192,1,128]{2,1,0:T(1,128)S(1)}, u32[]{:S(2)}, u32[]{:S(2)}) collective-permute-start(f32[192,1,128]{2,1,0:T(1,128)S(1)} %get-tuple-element.46), channel_id=1, source_target_pairs={{1,0},{0,1},{3,2},{2,3},{5,4},{4,5},{7,6},{6,7},{9,8},{8,9},{11,10... | collective-permute-start | bytes 294920 | tf_op jit(solution)/shard_map/ppermute | solution.py:28
  9.9 6.6 %copy-start = (f32[1,192,32,128]{3,2,1,0:T(8,128)S(1)}, f32[1,192,32,128]{3,2,1,0:T(8,128)}, u32[]{:S(2)}) copy-start(f32[1,192,32,128]{3,2,1,0:T(8,128)} %param.2) | copy-start | bytes 9437188
  16.5 3.9 %copy-start.5 = (f32[32,128]{1,0:T(8,128)S(1)}, f32[32,128]{1,0:T(8,128)}, u32[]{:S(2)}) copy-start(f32[32,128]{1,0:T(8,128)} %param.3) | copy-start | bytes 49156
  20.3 4.1 %copy-start.2 = (f32[192,32,127]{2,1,0:T(8,128)S(1)}, f32[192,32,127]{2,1,0:T(8,128)}, u32[]{:S(2)}) copy-start(f32[192,32,127]{2,1,0:T(8,128)} %get-tuple-element.41) | copy-start | bytes 9363460
  30.6 1.7 copy-start.1
  36.3 157.8 %all-reduce.6.cloned.1.call-start = ((), (), s32[]{:S(2)}) async-start(), calls=%async_computation.1 | async-start | bytes 262144 | tf_op jit(solution)/shard_map/psum | solution.py:160
  113.7 1.7 collective-permute-start.4
  113.7 1.6 collective-permute-start.5
  194.0 3.3 %copy-start.3 = (f32[4,32,128]{2,0,1:T(4,128)S(1)}, f32[4,32,128]{2,0,1:T(4,128)}, u32[]{:S(2)}) copy-start(f32[4,32,128]{2,0,1:T(4,128)} %get-tuple-element.7) | copy-start | bytes 196612
  194.0 3.3 %copy-start.4 = (f32[4,32,128]{2,0,1:T(4,128)S(1)}, f32[4,32,128]{2,0,1:T(4,128)}, u32[]{:S(2)}) copy-start(f32[4,32,128]{2,0,1:T(4,128)} %get-tuple-element.6) | copy-start | bytes 196612
  194.8 1.4 collective-permute-start
  194.8 1.4 collective-permute-start.1
  197.5 5.3 %collective-permute-start.6 = (f32[4,32,128]{2,0,1:T(4,128)S(1)}, f32[4,32,128]{2,0,1:T(4,128)S(1)}, u32[]{:S(2)}, u32[]{:S(2)}) collective-permute-start(f32[4,32,128]{2,0,1:T(4,128)S(1)} %get-tuple-element.23), channel_id=1, source_target_pairs={{0,16},{1,17},{2,18},{3,19},{4,20},{5,21},{6,22},{7,23},{8,24},{9,... | collective-permute-start | bytes 196616 | tf_op jit(solution)/shard_map/ppermute | solution.py:36
  202.8 1.2 collective-permute-start.7
  202.8 1.3 collective-permute-start.8
Sparse Core Ops, SparseCore 0:
  36.4 71.9 all-reduce.3
  123.3 70.6 all-reduce.5
where the time goes:
time: 218 us
  waiting for transfers between devices  145 us (67%)
  other arithmetic  21.1 us (10%)
  local copies, waits for them, and re-layouts  19.1 us (9%)
  between operations  14.5 us (7%)
  matrix products  11.8 us (5%)
  starting transfers between devices  5.8 us (3%)
    psum x2, waiting for transfers between devices, per_device(): distribution_array = lax.psum(moments(star, table), 'vel')  143 us
    slice x4, local copies, waits for them, and re-layouts, transport(): above = jnp.roll(field, -1, axis=2)  12.6 us
    dot_general x3, matrix products, moments(): jnp.dot(table, flat, precision=lax.Precision.HIGHEST, preferred_element_t...  11.8 us
    sub x2, other arithmetic, transport(): out - jnp.maximum(coef_y, 0.0) * (field - below)  10.1 us
  transfers between devices with their start and end apart: 11, of which 5 were waited for; matrix products, arithmetic and copies ran while one was open for 8% of the time, Pallas kernels for 0%

commit v1 on v0

v1 whole, which is shorter than its diff:
```python
import functools
import math

import jax
import jax.numpy as jnp
from jax import lax
from jax.experimental import pallas as pl
from jax.experimental.pallas import tpu as pltpu
from jax.sharding import PartitionSpec as P

NVX = 48
NVY = 32
HALF = NVY // 2
TILE = 8
vel_max = 6.0
fine_ratio = 0.075
coarse_ratio = 0.15
density_floor = 0.3
thermal_lower_bound = 0.3
DVX = 2.0 * vel_max / NVX
DVY = 2.0 * vel_max / NVY
WEIGHT = DVX * DVY / (2.0 * math.pi)
MESH = pl.DeviceIdType.MESH
f32 = jnp.float32


def physical_variables(u):
    rs = jnp.maximum(u[0], density_floor)
    ux = u[1] / rs
    uy = u[2] / rs
    temp = jnp.maximum((u[3] - 0.5 * (u[1] * ux + u[2] * uy)) / rs, thermal_lower_bound)
    return rs, ux, uy, temp


def chunk_of(first, c):
    k = first + c * HALF
    i = k // NVY
    j = k % NVY
    vx = -vel_max + (i.astype(f32) + 0.5) * DVX
    vy = -vel_max + (j.astype(f32) + 0.5) * DVY
    return vx, vy, j // HALF, j


def coarse(main, halo):
    nx = main.shape[1]
    rows = nx + 2 * TILE
    u = [jnp.concatenate([halo[0, c], main[c], halo[1, c]], axis=0) for c in range(4)]
    ny = u[0].shape[1]
    rs, ux, uy, temp = physical_variables(u)
    p = rs * temp
    wave = jnp.sqrt(2.0 * temp)
    fx = [u[1], u[1] * ux + p, u[2] * ux, (u[3] + p) * ux]
    fy = [u[2], u[1] * uy, u[2] * uy + p, (u[3] + p) * uy]
    sx = jnp.abs(ux) + wave
    sy = jnp.abs(uy) + wave
    mx = jnp.maximum(sx, pltpu.roll(sx, rows - 1, 0))
    my = jnp.maximum(sy, pltpu.roll(sy, ny - 1, 1))
    out = []
    for c in range(4):
        face_x = 0.5 * (fx[c] + pltpu.roll(fx[c], rows - 1, 0)) - 0.5 * mx * (
            pltpu.roll(u[c], rows - 1, 0) - u[c]
        )
        face_y = 0.5 * (fy[c] + pltpu.roll(fy[c], ny - 1, 1)) - 0.5 * my * (
            pltpu.roll(u[c], ny - 1, 1) - u[c]
        )
        g = u[c] - coarse_ratio * (
            face_x - pltpu.roll(face_x, 1, 0) + (face_y - pltpu.roll(face_y, 1, 1))
        )
        out.append(g[TILE : TILE + nx])
    return out


def advance_kernel(
    nw, nv, owners,
    f, r, star2, corr_out, e_out,
    fpad, spad, s2, rpad, part, red_in, full, uh, vfull, vh, corr, yt, flux, phys, delta,
    load_sem, halo_send, halo_recv, rs_send, rs_recv, ag_send, ag_recv, edge_send, edge_recv,
    win_send, win_recv, out_sem,
):
    w, v, s = lax.axis_index("win"), lax.axis_index("vel"), lax.axis_index("sp")
    count, nx, ny = f.shape
    chunks = count // HALF
    first = v * count
    other = 1 - s
    pos = (2 * v) // nv
    main = pl.ds(2 * TILE, nx)
    end = 2 * TILE + nx
    up = pl.ds(2 * TILE + 1 - 2 * pos, nx)
    hb = pl.multiple_of(end - (end - TILE) * pos, TILE)
    edge = pl.ds(hb, TILE)
    edge_up = pl.ds(hb + 1 - 2 * pos, TILE)
    band = 4 * nx // owners

    def peer(d):
        return lax.rem(v + d, nv)

    load_f = pltpu.make_async_copy(f, fpad.at[:, main], load_sem.at[0])
    load_r = pltpu.make_async_copy(r, rpad.at[main], load_sem.at[1])
    load_f.start()
    load_r.start()

    barrier = pltpu.get_barrier_semaphore()
    for d in range(1, nv):
        pl.semaphore_signal(barrier, inc=1, device_id=(w, peer(d), s), device_id_type=MESH)
    for d in range(nv):
        pl.semaphore_signal(barrier, inc=1, device_id=(w, peer(d), other), device_id_type=MESH)

    @pl.when(w + 1 < nw)
    def _():
        pl.semaphore_signal(barrier, inc=1, device_id=(w + 1, v, s), device_id_type=MESH)
        pl.semaphore_signal(barrier, inc=1, device_id=(w + 1, v, other), device_id_type=MESH)

    @pl.when(w > 0)
    def _():
        pl.semaphore_signal(barrier, inc=1, device_id=(w - 1, v, s), device_id_type=MESH)
        pl.semaphore_signal(barrier, inc=1, device_id=(w - 1, v, other), device_id_type=MESH)

    ends = jnp.where(w > 0, 2, 0) + jnp.where(w + 1 < nw, 2, 0)
    pl.semaphore_wait(barrier, 2 * nv - 1 + ends)

    def remote(src, dst, send, recv, device):
        return pltpu.make_async_remote_copy(
            src_ref=src, dst_ref=dst, send_sem=send, recv_sem=recv,
            device_id=device, device_id_type=MESH,
        )

    source = pl.ds(pl.multiple_of((nx - TILE) * pos, TILE), TILE)
    halos = [
        remote(f.at[:, source], fpad.at[:, edge], halo_send.at[0], halo_recv.at[0], (w, v, other)),
        remote(r.at[pl.ds(0, TILE)], rpad.at[pl.ds(end, TILE)], halo_send.at[1], halo_recv.at[1], (w, v, other)),
        remote(r.at[pl.ds(nx - TILE, TILE)], rpad.at[pl.ds(TILE, TILE)], halo_send.at[2], halo_recv.at[2], (w, v, other)),
    ]
    for copy in halos:
        copy.start()
    part[...] = jnp.zeros_like(part)
    load_f.wait()
    load_r.wait()
    for copy in halos:
        copy.wait()

    def add_moments(ph, vx, a0, a1, a2):
        part[ph, 0] += WEIGHT * a0
        part[ph, 1] += (WEIGHT * vx) * a0
        part[ph, 2] += WEIGHT * a1
        part[ph, 3] += (0.5 * WEIGHT) * (vx * vx * a0 + a2)

    @pl.loop(0, chunks)
    def _(c):
        vx, vy0, half, _j = chunk_of(first, c)
        shift = ny - 1 - (ny - 2) * half
        ca = fine_ratio * jnp.abs(vx)
        zero = jnp.zeros((nx, ny), f32)
        acc = [zero] * 6
        for jj in range(HALF):
            k = c * HALF + jj
            vy = vy0 + jj * DVY
            cb = fine_ratio * jnp.abs(vy)
            cc = 1.0 - ca - cb
            g = fpad[k, main]
            star = cc * g + ca * fpad[k, up] + cb * pltpu.roll(g, shift, 1)
            spad[k, main] = star
            h = fpad[k, edge]
            spad[k, edge] = cc * h + ca * fpad[k, edge_up] + cb * pltpu.roll(h, shift, 1)
            yg, ys = vy * g, vy * star
            acc = [acc[0] + star, acc[1] + ys, acc[2] + vy * ys, acc[3] + g, acc[4] + yg, acc[5] + vy * yg]
        add_moments(0, vx, *acc[:3])
        add_moments(1, vx, *acc[3:])

    def band_of(o):
        row = o * band
        return row // nx, pl.ds(pl.multiple_of(row % nx, TILE), band)

    def scatter(ph):
        for d in range(1, nv):
            def send(d=d):
                comp, rows = band_of(peer(d))
                remote(
                    part.at[ph, comp, rows], red_in.at[ph, d - 1], rs_send.at[ph], rs_recv.at[ph],
                    (w, peer(d), s),
                ).start()

            if owners == nv:
                send()
            else:
                pl.when(peer(d) < owners)(send)

    def owner(fn):
        if owners == nv:
            fn()
        else:
            pl.when(v < owners)(fn)

    def settle(ref, sem):
        pltpu.make_async_copy(ref, ref, sem).wait()

    def gather(ph):
        def go():
            settle(red_in.at[ph], rs_recv.at[ph])
            comp, rows = band_of(v)
            total = part[ph, comp, rows]
            for d in range(1, nv):
                total = total + red_in[ph, d - 1]
            full[ph, comp, rows] = total
            for d in range(1, nv):
                remote(
                    full.at[ph, comp, rows], full.at[ph, comp, rows], ag_send.at[ph], ag_recv.at[ph],
                    (w, peer(d), s),
                ).start()
            if ph < 2:
                row = (v * band) % nx

                @pl.when(row == 0)
                def _():
                    for d in range(nv):
                        remote(
                            full.at[ph, comp, pl.ds(0, TILE)], uh.at[ph, 1, comp],
                            edge_send.at[2 * ph], edge_recv.at[ph], (w, peer(d), other),
                        ).start()

                @pl.when(row + band == nx)
                def _():
                    for d in range(nv):
                        remote(
                            full.at[ph, comp, pl.ds(nx - TILE, TILE)], uh.at[ph, 0, comp],
                            edge_send.at[2 * ph + 1], edge_recv.at[ph], (w, peer(d), other),
                        ).start()

        owner(go)

    def gathered(ph):
        def mine():
            for _ in range(owners - 1):
                settle(red_in.at[ph, 0], ag_recv.at[ph])

        def all_of_them():
            for _ in range(owners):
                settle(red_in.at[ph, 0], ag_recv.at[ph])

        if owners == nv:
            settle(red_in.at[ph], ag_recv.at[ph])
        else:
            pl.when(v < owners)(mine)
            pl.when(v >= owners)(all_of_them)
        if ph < 2:
            settle(uh.at[ph], edge_recv.at[ph])

    scatter(0)
    scatter(1)

    rate = rpad[...]
    inv_main = 1.0 / (1.0 + rpad[main])
    inv_up = 1.0 / (1.0 + rpad[up])
    inv_edge = 1.0 / (1.0 + rpad[edge])

    @pl.loop(0, chunks)
    def _(c):
        vx, vy0, half, _j = chunk_of(first, c)
        shift = ny - 1 - (ny - 2) * half
        ca = fine_ratio * jnp.abs(vx)
        zero = jnp.zeros((nx, ny), f32)
        acc = [zero] * 3
        for jj in range(HALF):
            k = c * HALF + jj
            vy = vy0 + jj * DVY
            cb = fine_ratio * jnp.abs(vy)
            cc = 1.0 - ca - cb
            g = spad[k, main] * inv_main
            star = cc * g + (ca * spad[k, up]) * inv_up + cb * pltpu.roll(g, shift, 1)
            ys = vy * star
            acc = [acc[0] + star, acc[1] + ys, acc[2] + vy * ys]
        add_moments(2, vx, *acc)

    scatter(2)
    gather(0)
    gather(1)
    gather(2)

    gathered(0)
    wide = pl.ds(TILE, nx + 2 * TILE)
    u = [jnp.concatenate([uh[0, 0, c], full[0, c], uh[0, 1, c]], axis=0) for c in range(4)]
    rs, ux, uy, temp = physical_variables(u)
    rate = rpad[wide]
    phys[0, wide] = ux
    phys[1, wide] = uy
    phys[2, wide] = -0.5 / temp
    phys[3, wide] = rs / temp * (rate / (1.0 + rate))

    @pl.loop(1, 3 + nx // TILE)
    def _(t):
        rows = pl.ds(pl.multiple_of(t * TILE, TILE), TILE)
        ux, uy, scale, amp = [phys[n, rows] for n in range(4)]
        zero = jnp.zeros_like(ux)

        def half_sums(speeds, drift, keep):
            sums = {0: [zero] * 4, 1: [zero] * 4}
            for n, speed in enumerate(speeds):
                d = speed - drift
                e = jnp.exp(d * d * scale)
                if keep:
                    yt[n, rows] = e
                side = sums[int(speed > 0)]
                e1 = speed * e
                e2 = speed * e1
                sums[int(speed > 0)] = [side[0] + e, side[1] + e1, side[2] + e2, side[3] + speed * e2]
            return sums[1], sums[0]

        xp, xm = half_sums([-vel_max + (i + 0.5) * DVX for i in range(NVX)], ux, False)
        yp, ym = half_sums([-vel_max + (j + 0.5) * DVY for j in range(NVY)], uy, True)
        xs = [a + b for a, b in zip(xp, xm)]
        ys = [a + b for a, b in zip(yp, ym)]
        amp = WEIGHT * amp

        def store(n, coef, x, y):
            x = [coef * amp * t for t in x]
            flux[n, rows] = x[0] * y[0]
            flux[n + 1, rows] = x[1] * y[0]
            flux[n + 2, rows] = x[0] * y[1]
            flux[n + 3, rows] = 0.5 * (x[2] * y[0] + x[0] * y[2])

        store(0, 1.0, xs, ys)
        store(4, fine_ratio, xp[1:], ys)
        store(8, -fine_ratio, xm[1:], ys)
        store(12, fine_ratio, xs, yp[1:])
        store(16, -fine_ratio, xs, ym[1:])

    gathered(2)
    below, above = pl.ds(2 * TILE - 1, nx), pl.ds(2 * TILE + 1, nx)
    for c in range(4):
        to_y, from_y = flux[12 + c, main], flux[16 + c, main]
        e_out[c] = full[2, c] + (
            flux[c, main] - flux[4 + c, main] - flux[8 + c, main] - to_y - from_y
            + flux[4 + c, below] + flux[8 + c, above]
            + pltpu.roll(to_y, 1, 1) + pltpu.roll(from_y, ny - 1, 1)
        )
    gathered(1)
    stepped = coarse(full.at[1], uh.at[1])
    for c in range(4):
        delta[c] = e_out[c] - stepped[c]

    def onward(n):
        return [
            remote(corr, vfull, win_send.at[0], win_recv.at[0], (n, v, s)),
            remote(corr.at[:, pl.ds(0, TILE)], vh.at[1], win_send.at[1], win_recv.at[1], (n, v, other)),
            remote(corr.at[:, pl.ds(nx - TILE, TILE)], vh.at[0], win_send.at[2], win_recv.at[2], (n, v, other)),
        ]

    def pass_on():
        @pl.when(w + 1 < nw)
        def _():
            for copy in onward(w + 1):
                copy.start()

    @pl.when(w == 0)
    def _():
        for c in range(4):
            corr[c] = stepped[c] + delta[c]
        pass_on()

    @pl.loop(0, chunks)
    def _(c):
        vx, vy0, half, j0 = chunk_of(first, c)
        shift = ny - 1 - (ny - 2) * half
        ca = fine_ratio * jnp.abs(vx)
        dm = vx - phys[0, main]
        xm = phys[3, main] * jnp.exp(dm * dm * phys[2, main])
        de = vx - phys[0, edge]
        xe = phys[3, edge] * jnp.exp(de * de * phys[2, edge])
        for jj in range(HALF):
            k = c * HALF + jj
            fpad[k, main] = spad[k, main] * inv_main + xm * yt[j0 + jj, main]
            fpad[k, edge] = spad[k, edge] * inv_edge + xe * yt[j0 + jj, edge]
        for jj in range(HALF):
            k = c * HALF + jj
            cb = fine_ratio * jnp.abs(vy0 + jj * DVY)
            g = fpad[k, main]
            s2[k] = (1.0 - ca - cb) * g + ca * fpad[k, up] + cb * pltpu.roll(g, shift, 1)

    save = pltpu.make_async_copy(s2, star2, out_sem)
    save.start()

    @pl.when(w > 0)
    def _():
        for copy in onward(w):
            copy.wait_recv()
        moved = coarse(vfull, vh)
        for c in range(4):
            corr[c] = moved[c] + delta[c]
        pass_on()

    corr_out[...] = corr[...]
    save.wait()

    @pl.when(w + 1 < nw)
    def _():
        for copy in onward(w + 1):
            copy.wait_send()

    for ph in range(3):
        if owners == nv:
            settle(red_in.at[ph], rs_send.at[ph])
            settle(red_in.at[ph], ag_send.at[ph])
        else:
            for d in range(1, nv):
                @pl.when(peer(d) < owners)
                def _():
                    settle(red_in.at[ph, 0], rs_send.at[ph])

            def sent():
                settle(red_in.at[ph], ag_send.at[ph])

            pl.when(v < owners)(sent)

    def edges():
        row = (v * band) % nx
        for ph in range(2):
            for side, at_edge in ((0, row == 0), (1, row + band == nx)):
                @pl.when(at_edge)
                def _():
                    for _ in range(nv):
                        settle(uh.at[ph, 0, 0], edge_send.at[2 * ph + side])

    owner(edges)


def lift_kernel(star2, corr, ending, r, lifted, corrected, ye, yc, ph):
    count = star2.shape[0]
    step = pl.program_id(0)
    first = lax.axis_index("vel") * (count * pl.num_programs(0)) + step * count

    @pl.when(step == 0)
    def _():
        corrected[...] = corr[...]
        inv = 1.0 / (1.0 + r[...])
        ph[8] = inv
        for n, (u, table) in enumerate(((ending, ye), (corr, yc))):
            rs, ux, uy, temp = physical_variables(u)
            scale = -0.5 / temp
            amp = rs / temp
            ph[4 * n] = ux
            ph[4 * n + 1] = scale
            ph[4 * n + 2] = amp * inv if n == 0 else amp
            for j in range(NVY):
                d = (-vel_max + (j + 0.5) * DVY) - uy
                table[j] = jnp.exp(d * d * scale)

    inv = ph[8]
    for c in range(count // HALF):
        vx, _vy, _half, j0 = chunk_of(first, c)
        de, dc = vx - ph[0], vx - ph[4]
        xe = ph[2] * jnp.exp(de * de * ph[1])
        xc = ph[6] * jnp.exp(dc * dc * ph[5])
        for jj in range(HALF):
            k = c * HALF + jj
            lifted[k] = star2[k] * inv - xe * ye[j0 + jj] + xc * yc[j0 + jj]


def per_device(nw, nv, f_start, relax_rate):
    field = f_start[0]
    count, nx, ny = field.shape
    owners = min(nv, 4 * nx // TILE)
    band = 4 * nx // owners
    pad = nx + 4 * TILE
    vmem = pltpu.VMEM
    dma = pltpu.SemaphoreType.DMA
    small = jax.ShapeDtypeStruct((4, nx, ny), f32)
    in_vmem = pl.BlockSpec(memory_space=pltpu.VMEM)
    anywhere = pl.BlockSpec(memory_space=pl.ANY)
    star2, corr, ending = pl.pallas_call(
        functools.partial(advance_kernel, nw, nv, owners),
        out_shape=(jax.ShapeDtypeStruct((count, nx, ny), f32), small, small),
        in_specs=[anywhere, anywhere],
        out_specs=(anywhere, in_vmem, in_vmem),
        scratch_shapes=[
            vmem((count, pad, ny), f32),
            vmem((count, pad, ny), f32),
            vmem((count, nx, ny), f32),
            vmem((pad, ny), f32),
            vmem((3, 4, nx, ny), f32),
            vmem((3, nv - 1, band, ny), f32),
            vmem((3, 4, nx, ny), f32),
            vmem((2, 2, 4, TILE, ny), f32),
            vmem((4, nx, ny), f32),
            vmem((2, 4, TILE, ny), f32),
            vmem((4, nx, ny), f32),
            vmem((NVY, pad, ny), f32),
            vmem((20, pad, ny), f32),
            vmem((4, pad, ny), f32),
            vmem((4, nx, ny), f32),
            dma((2,)), dma((3,)), dma((3,)), dma((3,)), dma((3,)), dma((3,)), dma((3,)),
            dma((4,)), dma((2,)), dma((3,)), dma((3,)), dma,
        ],
        compiler_params=pltpu.CompilerParams(
            collective_id=0, has_side_effects=True, vmem_limit_bytes=40 << 20
        ),
        name="advance",
    )(field, relax_rate)

    block = 2 * HALF if count % (2 * HALF) == 0 else HALF
    whole = pl.BlockSpec((4, nx, ny), lambda i: (0, 0, 0))
    slab = pl.BlockSpec((block, nx, ny), lambda i: (i, 0, 0))
    lifted, corrected = pl.pallas_call(
        lift_kernel,
        grid=(count // block,),
        out_shape=(jax.ShapeDtypeStruct((count, nx, ny), f32), small),
        in_specs=[slab, whole, whole, pl.BlockSpec((nx, ny), lambda i: (0, 0))],
        out_specs=(slab, whole),
        scratch_shapes=[vmem((NVY, nx, ny), f32), vmem((NVY, nx, ny), f32), vmem((9, nx, ny), f32)],
        name="lift",
    )(star2, corr, ending, relax_rate)
    return corrected[None], lifted[None]


def solution(mesh):
    return jax.shard_map(
        functools.partial(per_device, mesh.shape["win"], mesh.shape["vel"]),
        mesh=mesh,
        in_specs=(P("win", "vel", "sp", None), P("sp", None)),
        out_specs=(P("win", None, "sp", None), P("win", "vel", "sp", None)),
        check_vma=False,
    )
```

time: 218 us -> 38.1 us (0.17)
  waiting for transfers between devices: 145 us -> 0 us
  Pallas kernels: 0 us -> 31.6 us
  other arithmetic: 21.1 us -> 0 us
  between operations: 14.5 us -> 0.66 us
  local copies, waits for them, and re-layouts: 19.1 us -> 5.48 us
  matrix products: 11.8 us -> 0 us
  starting transfers between devices: 5.8 us -> 0 us
    psum x2 -> x0, waiting for transfers between devices: 143 us -> none  [per_device(): distribution_array = lax.psum(moments(star, table), 'vel')]
    pallas_call x0 -> x2, Pallas kernels: none -> 31.6 us  [the longest x1 25.9 us: per_device(): pl.pallas_call(functools.partial(advance_kernel, nw, nv, owners), out_sha...]
    slice x10 -> x0, local copies, waits for them, and re-layouts: 15.9 us -> none  [the longest x4 12.6 us: transport(): above = jnp.roll(field, -1, axis=2)]
    dot_general x3 -> x0, matrix products: 11.8 us -> none  [moments(): jnp.dot(table, flat, precision=lax.Precision.HIGHEST, preferred_element_t...]
    sub x6 -> x0, other arithmetic: 10.9 us -> none  [the longest x2 10.1 us: transport(): out - jnp.maximum(coef_y, 0.0) * (field - below)]
    ppermute x9 -> x0, starting transfers between devices: 5.54 us -> none  [the longest x1 3.38 us: shifted(): lax.ppermute(value, axis, [(source, source + steps) for source in range(l...]
    div x4 -> x0, other arithmetic: 4.2 us -> none  [the longest x1 2.93 us: per_device(): (star + rates * equilibrium_density(distribution_array, vel_x, vel_y)) /...]
    broadcast_in_dim x1 -> x0, other arithmetic: 3.83 us -> none  [per_device(): return (result[None], lifted[None])]
  transfers between devices with their start and end apart: 11 -> 0, of which waited for: 5 -> 0; matrix products, arithmetic and copies ran while one was open for 8% -> 0% of each run, Pallas kernels for 0% -> 0%
where the time goes in v1:
time: 38.1 us; the launch traced here: 37.8 us
  Pallas kernels  31.6 us (83%)
  local copies, waits for them, and re-layouts  5.48 us (14%)
  between operations  0.66 us (2%)
    pallas_call x1, Pallas kernels, per_device(): pl.pallas_call(functools.partial(advance_kernel, nw, nv, owners), out_sha...  25.9 us
    pallas_call x1, Pallas kernels, per_device(): pl.pallas_call(lift_kernel, grid=(count // block,), out_shape=(jax.ShapeD...  5.69 us
    unnamed x10, local copies, waits for them, and re-layouts  5.48 us

profile of v1, /device:TPU:0, one launch (start us, length us, event | category | flops | bytes accessed | tf_op | source)
XLA Modules:
  0.0 37.8 jit_solution(8973132364926202222)
XLA Ops:
  0.6 0.0 copy-start
  0.6 1.9 %copy-done = f32[1,192,32,128]{3,2,1,0:T(8,128)S(1)} copy-done((f32[1,192,32,128]{3,2,1,0:T(8,128)S(1)}, f32[1,192,32,128]{3,2,1,0:T(8,128)}, u32[]{:S(2)}) %copy-start) | copy-done | bytes 3145752
  2.5 0.0 copy-start.2
  2.5 0.7 %copy-done.2 = f32[32,128]{1,0:T(8,128)S(1)} copy-done((f32[32,128]{1,0:T(8,128)S(1)}, f32[32,128]{1,0:T(8,128)}, u32[]{:S(2)}) %copy-start.2) | copy-done | bytes 16408
  3.2 25.9 %advance.1 = (f32[192,32,128]{2,1,0:T(8,128)S(1)}, f32[4,32,128]{2,1,0:T(8,128)S(1)}, f32[4,32,128]{2,1,0:T(8,128)S(1)}) custom-call(f32[192,32,128]{2,1,0:T(8,128)S(1)} %bitcast.3, f32[32,128]{1,0:T(8,128)S(1)} %copy-done.2), custom_call_target="tpu_custom_call" | custom-call | tf_op jit(solution)/shard_map/advance/pallas_call | solution.py:468
  29.2 0.0 copy-start.1
  29.2 1.6 %copy-done.1 = f32[192,32,128]{2,1,0:T(8,128)} copy-done((f32[192,32,128]{2,1,0:T(8,128)}, f32[192,32,128]{2,1,0:T(8,128)S(1)}, u32[]{:S(2)}) %copy-start.1) | copy-done | bytes 3145752
  30.8 0.0 copy-start.3
  30.8 0.6 %copy-done.3 = f32[4,32,128]{2,1,0:T(8,128)} copy-done((f32[4,32,128]{2,1,0:T(8,128)}, f32[4,32,128]{2,1,0:T(8,128)S(1)}, u32[]{:S(2)}) %copy-start.3) | copy-done | bytes 65560
  31.5 0.0 copy-start.4
  31.5 0.6 %copy-done.4 = f32[4,32,128]{2,1,0:T(8,128)} copy-done((f32[4,32,128]{2,1,0:T(8,128)}, f32[4,32,128]{2,1,0:T(8,128)S(1)}, u32[]{:S(2)}) %copy-start.4) | copy-done | bytes 65560
  32.1 5.7 %lift.1 = (f32[192,32,128]{2,1,0:T(8,128)}, f32[4,32,128]{2,1,0:T(8,128)}) custom-call(f32[192,32,128]{2,1,0:T(8,128)} %copy-done.1, f32[4,32,128]{2,1,0:T(8,128)} %copy-done.3, f32[4,32,128]{2,1,0:T(8,128)} %copy-done.4, f32[32,128]{1,0:T(8,128)} %r.3), custom_call_target="tpu_custom_call" | custom-call | tf_op jit(solution)/shard_map/lift/pallas_call | solution.py:501
Async XLA Ops:
  0.6 1.9 %copy-start = (f32[1,192,32,128]{3,2,1,0:T(8,128)S(1)}, f32[1,192,32,128]{3,2,1,0:T(8,128)}, u32[]{:S(2)}) copy-start(f32[1,192,32,128]{3,2,1,0:T(8,128)} %param.2) | copy-start | bytes 9437188
  2.5 0.7 %copy-start.2 = (f32[32,128]{1,0:T(8,128)S(1)}, f32[32,128]{1,0:T(8,128)}, u32[]{:S(2)}) copy-start(f32[32,128]{1,0:T(8,128)} %r.3) | copy-start | bytes 49156
  29.2 1.7 %copy-start.1 = (f32[192,32,128]{2,1,0:T(8,128)}, f32[192,32,128]{2,1,0:T(8,128)S(1)}, u32[]{:S(2)}) copy-start(f32[192,32,128]{2,1,0:T(8,128)S(1)} %get-tuple-element.7.star2) | copy-start | bytes 9437188
  30.8 0.6 %copy-start.3 = (f32[4,32,128]{2,1,0:T(8,128)}, f32[4,32,128]{2,1,0:T(8,128)S(1)}, u32[]{:S(2)}) copy-start(f32[4,32,128]{2,1,0:T(8,128)S(1)} %get-tuple-element.8.corr) | copy-start | bytes 196612
  31.5 0.6 %copy-start.4 = (f32[4,32,128]{2,1,0:T(8,128)}, f32[4,32,128]{2,1,0:T(8,128)S(1)}, u32[]{:S(2)}) copy-start(f32[4,32,128]{2,1,0:T(8,128)S(1)} %get-tuple-element.9.ending) | copy-start | bytes 196612

commit v2 on v1

--- a/solution.py
+++ b/solution.py
@@ -73,9 +73,9 @@
 def advance_kernel(
     nw, nv, owners,
     f, r, star2, corr_out, e_out,
-    fpad, spad, s2, rpad, part, red_in, full, uh, vfull, vh, corr, yt, flux, phys, delta,
+    fpad, spad, rpad, part, red_in, full, uh, vfull, vh, corr, yt, flux, phys, delta,
     load_sem, halo_send, halo_recv, rs_send, rs_recv, ag_send, ag_recv, edge_send, edge_recv,
-    win_send, win_recv, out_sem,
+    win_send, win_recv,
 ):
     w, v, s = lax.axis_index("win"), lax.axis_index("vel"), lax.axis_index("sp")
     count, nx, ny = f.shape
@@ -373,10 +373,7 @@
             k = c * HALF + jj
             cb = fine_ratio * jnp.abs(vy0 + jj * DVY)
             g = fpad[k, main]
-            s2[k] = (1.0 - ca - cb) * g + ca * fpad[k, up] + cb * pltpu.roll(g, shift, 1)
-
-    save = pltpu.make_async_copy(s2, star2, out_sem)
-    save.start()
+            star2[k] = (1.0 - ca - cb) * g + ca * fpad[k, up] + cb * pltpu.roll(g, shift, 1)
 
     @pl.when(w > 0)
     def _():
@@ -388,7 +385,6 @@
         pass_on()
 
     corr_out[...] = corr[...]
-    save.wait()
 
     @pl.when(w + 1 < nw)
     def _():
@@ -422,36 +418,44 @@
     owner(edges)
 
 
-def lift_kernel(star2, corr, ending, r, lifted, corrected, ye, yc, ph):
+def lift_kernel(parts, star2, corr, ending, r, lifted, corrected, ye, yc, out, save_sem):
     count = star2.shape[0]
-    step = pl.program_id(0)
-    first = lax.axis_index("vel") * (count * pl.num_programs(0)) + step * count
-
-    @pl.when(step == 0)
-    def _():
-        corrected[...] = corr[...]
-        inv = 1.0 / (1.0 + r[...])
-        ph[8] = inv
-        for n, (u, table) in enumerate(((ending, ye), (corr, yc))):
-            rs, ux, uy, temp = physical_variables(u)
-            scale = -0.5 / temp
-            amp = rs / temp
-            ph[4 * n] = ux
-            ph[4 * n + 1] = scale
-            ph[4 * n + 2] = amp * inv if n == 0 else amp
-            for j in range(NVY):
-                d = (-vel_max + (j + 0.5) * DVY) - uy
-                table[j] = jnp.exp(d * d * scale)
-
-    inv = ph[8]
-    for c in range(count // HALF):
-        vx, _vy, _half, j0 = chunk_of(first, c)
-        de, dc = vx - ph[0], vx - ph[4]
-        xe = ph[2] * jnp.exp(de * de * ph[1])
-        xc = ph[6] * jnp.exp(dc * dc * ph[5])
-        for jj in range(HALF):
-            k = c * HALF + jj
-            lifted[k] = star2[k] * inv - xe * ye[j0 + jj] + xc * yc[j0 + jj]
+    first = lax.axis_index("vel") * count
+    corrected[...] = corr[...]
+    inv = 1.0 / (1.0 + r[...])
+    sides = []
+    for u, table in ((ending, ye), (corr, yc)):
+        rs, ux, uy, temp = physical_variables(u)
+        scale = -0.5 / temp
+        amp = rs / temp
+        sides.append((ux, scale, amp))
+        for j in range(NVY):
+            d = (-vel_max + (j + 0.5) * DVY) - uy
+            table[j] = jnp.exp(d * d * scale)
+    (ue, se, me), (uc, sc, mc) = sides
+    me = me * inv
+    chunks = count // HALF
+    per = chunks // parts
+
+    def save(n):
+        rows = pl.ds(n * per * HALF, per * HALF)
+        return pltpu.make_async_copy(out.at[rows], lifted.at[rows], save_sem.at[n])
+
+    for n in range(parts):
+
+        @pl.loop(n * per, (n + 1) * per)
+        def _(c):
+            vx, _vy, _half, j0 = chunk_of(first, c)
+            de, dc = vx - ue, vx - uc
+            xe = me * jnp.exp(de * de * se)
+            xc = mc * jnp.exp(dc * dc * sc)
+            for jj in range(HALF):
+                k = c * HALF + jj
+                out[k] = star2[k] * inv - xe * ye[j0 + jj] + xc * yc[j0 + jj]
+
+        save(n).start()
+    for n in range(parts):
+        save(n).wait()
 
 
 def per_device(nw, nv, f_start, relax_rate):
@@ -464,16 +468,16 @@
     dma = pltpu.SemaphoreType.DMA
     small = jax.ShapeDtypeStruct((4, nx, ny), f32)
     in_vmem = pl.BlockSpec(memory_space=pltpu.VMEM)
-    anywhere = pl.BlockSpec(memory_space=pl.ANY)
+    in_hbm = pl.BlockSpec(memory_space=pltpu.HBM)
+    field = pltpu.with_memory_space_constraint(field, pltpu.HBM)
     star2, corr, ending = pl.pallas_call(
         functools.partial(advance_kernel, nw, nv, owners),
         out_shape=(jax.ShapeDtypeStruct((count, nx, ny), f32), small, small),
-        in_specs=[anywhere, anywhere],
-        out_specs=(anywhere, in_vmem, in_vmem),
+        in_specs=[in_hbm, in_hbm],
+        out_specs=(in_vmem, in_vmem, in_vmem),
         scratch_shapes=[
             vmem((count, pad, ny), f32),
             vmem((count, pad, ny), f32),
-            vmem((count, nx, ny), f32),
             vmem((pad, ny), f32),
             vmem((3, 4, nx, ny), f32),
             vmem((3, nv - 1, band, ny), f32),
@@ -487,24 +491,25 @@
             vmem((4, pad, ny), f32),
             vmem((4, nx, ny), f32),
             dma((2,)), dma((3,)), dma((3,)), dma((3,)), dma((3,)), dma((3,)), dma((3,)),
-            dma((4,)), dma((2,)), dma((3,)), dma((3,)), dma,
+            dma((4,)), dma((2,)), dma((3,)), dma((3,)),
         ],
         compiler_params=pltpu.CompilerParams(
             collective_id=0, has_side_effects=True, vmem_limit_bytes=40 << 20
         ),
         name="advance",
-    )(field, relax_rate)
-
-    block = 2 * HALF if count % (2 * HALF) == 0 else HALF
-    whole = pl.BlockSpec((4, nx, ny), lambda i: (0, 0, 0))
-    slab = pl.BlockSpec((block, nx, ny), lambda i: (i, 0, 0))
+    )(field, pltpu.with_memory_space_constraint(relax_rate, pltpu.HBM))
+
+    chunks = count // HALF
+    parts = next(n for n in (6, 4, 3, 2, 1) if chunks % n == 0)
     lifted, corrected = pl.pallas_call(
-        lift_kernel,
-        grid=(count // block,),
+        functools.partial(lift_kernel, parts),
         out_shape=(jax.ShapeDtypeStruct((count, nx, ny), f32), small),
-        in_specs=[slab, whole, whole, pl.BlockSpec((nx, ny), lambda i: (0, 0))],
-        out_specs=(slab, whole),
-        scratch_shapes=[vmem((NVY, nx, ny), f32), vmem((NVY, nx, ny), f32), vmem((9, nx, ny), f32)],
+        in_specs=[in_vmem] * 4,
+        out_specs=(in_hbm, in_vmem),
+        scratch_shapes=[
+            vmem((NVY, nx, ny), f32), vmem((NVY, nx, ny), f32), vmem((count, nx, ny), f32), dma((parts,)),
+        ],
+        compiler_params=pltpu.CompilerParams(vmem_limit_bytes=16 << 20),
         name="lift",
     )(star2, corr, ending, relax_rate)
     return corrected[None], lifted[None]

time: 38.1 us -> 29 us (0.76)
  local copies, waits for them, and re-layouts: 5.48 us -> 0.01 us
  Pallas kernels: 31.6 us -> 28.2 us
    unnamed x10 -> x2, local copies, waits for them, and re-layouts: 5.48 us -> 0.01 us
    pallas_call x1, Pallas kernels: 5.69 us -> 2.68 us  [per_device(): pl.pallas_call(functools.partial(lift_kernel, parts), out_shape=(jax.Shap...]
    pallas_call x1, Pallas kernels: 25.9 us -> 25.5 us  [per_device(): pl.pallas_call(functools.partial(advance_kernel, nw, nv, owners), out_sha...]
where the time goes in v2:
time: 29 us; the launch traced here: 28.9 us
  Pallas kernels  28.2 us (97%)
  between operations  0.65 us (2%)
    pallas_call x1, Pallas kernels, per_device(): pl.pallas_call(functools.partial(advance_kernel, nw, nv, owners), out_sha...  25.5 us
    pallas_call x1, Pallas kernels, per_device(): pl.pallas_call(functools.partial(lift_kernel, parts), out_shape=(jax.Shap...  2.68 us

profile of v2, /device:TPU:0, one launch (start us, length us, event | category | flops | bytes accessed | tf_op | source)
XLA Modules:
  0.0 28.9 jit_solution(2233797246017794707)
XLA Ops:
  0.6 0.0 copy-start
  0.6 25.5 %advance.1 = (f32[192,32,128]{2,1,0:T(8,128)S(1)}, f32[4,32,128]{2,1,0:T(8,128)S(1)}, f32[4,32,128]{2,1,0:T(8,128)S(1)}) custom-call(f32[192,32,128]{2,1,0:T(8,128)} %bitcast.3, f32[32,128]{1,0:T(8,128)} %r.3), custom_call_target="tpu_custom_call" | custom-call | tf_op jit(solution)/shard_map/advance/pallas_call | solution.py:473
  26.2 0.0 copy-done
  26.2 2.7 %lift.1 = (f32[192,32,128]{2,1,0:T(8,128)}, f32[4,32,128]{2,1,0:T(8,128)}) custom-call(f32[192,32,128]{2,1,0:T(8,128)S(1)} %get-tuple-element.7.star2, f32[4,32,128]{2,1,0:T(8,128)S(1)} %get-tuple-element.8.corr, f32[4,32,128]{2,1,0:T(8,128)S(1)} %get-tuple-element.9.ending, f32[32,128]{1,0:T(8,128)S(1)} %copy-done), custom_call_target="tpu_custom_call" | custom-call | tf_op jit(solution)/shard_map/lift/pallas_call | solution.py:504
Async XLA Ops:
  0.6 25.5 %copy-start = (f32[32,128]{1,0:T(8,128)S(1)}, f32[32,128]{1,0:T(8,128)}, u32[]{:S(2)}) copy-start(f32[32,128]{1,0:T(8,128)} %r.3) | copy-start | bytes 49156

commit v3 on v2

--- a/solution.py
+++ b/solution.py
@@ -22,6 +22,8 @@
 WEIGHT = DVX * DVY / (2.0 * math.pi)
 MESH = pl.DeviceIdType.MESH
 f32 = jnp.float32
+ORDERS = [(p, q) for p in range(5) for q in range(5 - p)]
+PLACE = {order: n for n, order in enumerate(ORDERS)}
 
 
 def physical_variables(u):
@@ -73,7 +75,7 @@
 def advance_kernel(
     nw, nv, owners,
     f, r, star2, corr_out, e_out,
-    fpad, spad, rpad, part, red_in, full, uh, vfull, vh, corr, yt, flux, phys, delta,
+    fpad, spad, rpad, bsum, hsum, part, red_in, full, uh, vfull, vh, corr, yt, flux, phys, delta,
     load_sem, halo_send, halo_recv, rs_send, rs_recv, ag_send, ag_recv, edge_send, edge_recv,
     win_send, win_recv,
 ):
@@ -115,56 +117,11 @@
         pl.semaphore_signal(barrier, inc=1, device_id=(w - 1, v, s), device_id_type=MESH)
         pl.semaphore_signal(barrier, inc=1, device_id=(w - 1, v, other), device_id_type=MESH)
 
-    ends = jnp.where(w > 0, 2, 0) + jnp.where(w + 1 < nw, 2, 0)
-    pl.semaphore_wait(barrier, 2 * nv - 1 + ends)
-
     def remote(src, dst, send, recv, device):
         return pltpu.make_async_remote_copy(
             src_ref=src, dst_ref=dst, send_sem=send, recv_sem=recv,
             device_id=device, device_id_type=MESH,
         )
-
-    source = pl.ds(pl.multiple_of((nx - TILE) * pos, TILE), TILE)
-    halos = [
-        remote(f.at[:, source], fpad.at[:, edge], halo_send.at[0], halo_recv.at[0], (w, v, other)),
-        remote(r.at[pl.ds(0, TILE)], rpad.at[pl.ds(end, TILE)], halo_send.at[1], halo_recv.at[1], (w, v, other)),
-        remote(r.at[pl.ds(nx - TILE, TILE)], rpad.at[pl.ds(TILE, TILE)], halo_send.at[2], halo_recv.at[2], (w, v, other)),
-    ]
-    for copy in halos:
-        copy.start()
-    part[...] = jnp.zeros_like(part)
-    load_f.wait()
-    load_r.wait()
-    for copy in halos:
-        copy.wait()
-
-    def add_moments(ph, vx, a0, a1, a2):
-        part[ph, 0] += WEIGHT * a0
-        part[ph, 1] += (WEIGHT * vx) * a0
-        part[ph, 2] += WEIGHT * a1
-        part[ph, 3] += (0.5 * WEIGHT) * (vx * vx * a0 + a2)
-
-    @pl.loop(0, chunks)
-    def _(c):
-        vx, vy0, half, _j = chunk_of(first, c)
-        shift = ny - 1 - (ny - 2) * half
-        ca = fine_ratio * jnp.abs(vx)
-        zero = jnp.zeros((nx, ny), f32)
-        acc = [zero] * 6
-        for jj in range(HALF):
-            k = c * HALF + jj
-            vy = vy0 + jj * DVY
-            cb = fine_ratio * jnp.abs(vy)
-            cc = 1.0 - ca - cb
-            g = fpad[k, main]
-            star = cc * g + ca * fpad[k, up] + cb * pltpu.roll(g, shift, 1)
-            spad[k, main] = star
-            h = fpad[k, edge]
-            spad[k, edge] = cc * h + ca * fpad[k, edge_up] + cb * pltpu.roll(h, shift, 1)
-            yg, ys = vy * g, vy * star
-            acc = [acc[0] + star, acc[1] + ys, acc[2] + vy * ys, acc[3] + g, acc[4] + yg, acc[5] + vy * yg]
-        add_moments(0, vx, *acc[:3])
-        add_moments(1, vx, *acc[3:])
 
     def band_of(o):
         row = o * band
@@ -244,35 +201,123 @@
         if ph < 2:
             settle(uh.at[ph], edge_recv.at[ph])
 
+    load_f.wait()
+    parity = (first // HALF) % 2
+    rounds = (chunks + 1) // 2
+
+    @pl.loop(0, nx // TILE)
+    def _(t):
+        rows = pl.ds(pl.multiple_of(2 * TILE + t * TILE, TILE), TILE)
+        for h in range(2):
+            acc = {order: jnp.zeros((TILE, ny), f32) for order in ORDERS}
+            for n in range(rounds):
+                c = (h + parity) % 2 + 2 * n
+                weight = 1.0
+                if chunks % 2:
+                    weight = jnp.where(c < chunks, 1.0, 0.0).astype(f32)
+                    c = jnp.minimum(c, chunks - 1)
+                vx = chunk_of(first, c)[0]
+                sums = [jnp.zeros((TILE, ny), f32)] * 5
+                for jj in range(HALF // 2, HALF):
+                    tt = (jj + 0.5) * DVY - 0.5 * vel_max
+                    high = fpad[c * HALF + jj, rows]
+                    low = fpad[c * HALF + HALF - 1 - jj, rows]
+                    even, odd = high + low, high - low
+                    sums = [
+                        sums[0] + even, sums[1] + tt * odd, sums[2] + tt**2 * even,
+                        sums[3] + tt**3 * odd, sums[4] + tt**4 * even,
+                    ]
+                power = weight
+                for q in range(5):
+                    for m in range(5 - q):
+                        term = sums[m] if q == 0 and chunks % 2 == 0 else sums[m] * power
+                        acc[m, q] = acc[m, q] + term
+                    power = power * vx
+            centre = (h - 0.5) * vel_max
+            for p, q in ORDERS:
+                total = acc[p, q]
+                for m in range(p):
+                    total = total + (math.comb(p, m) * centre ** (p - m)) * acc[m, q]
+                bsum[h, PLACE[p, q], rows] = total
+
+    def components(ph, get):
+        part[ph, 0] = WEIGHT * get(0, 0)
+        part[ph, 1] = WEIGHT * get(0, 1)
+        part[ph, 2] = WEIGHT * get(1, 0)
+        part[ph, 3] = (0.5 * WEIGHT) * (get(0, 2) + get(2, 0))
+
+    components(1, lambda p, q: bsum[0, PLACE[p, q], main] + bsum[1, PLACE[p, q], main])
+
+    ends = jnp.where(w > 0, 2, 0) + jnp.where(w + 1 < nw, 2, 0)
+    pl.semaphore_wait(barrier, 2 * nv - 1 + ends)
+    load_r.wait()
+
+    source = pl.ds(pl.multiple_of((nx - TILE) * pos, TILE), TILE)
+    kept = pl.ds(pl.multiple_of(2 * TILE + (nx - TILE) * pos, TILE), TILE)
+    halos = [
+        remote(bsum.at[:, :, kept], bsum.at[:, :, edge], halo_send.at[3], halo_recv.at[3], (w, v, other)),
+        remote(r.at[pl.ds(0, TILE)], rpad.at[pl.ds(end, TILE)], halo_send.at[1], halo_recv.at[1], (w, v, other)),
+        remote(r.at[pl.ds(nx - TILE, TILE)], rpad.at[pl.ds(TILE, TILE)], halo_send.at[2], halo_recv.at[2], (w, v, other)),
+        remote(f.at[:, source], fpad.at[:, edge], halo_send.at[0], halo_recv.at[0], (w, v, other)),
+    ]
+    for copy in halos:
+        copy.start()
+    scatter(1)
+    for copy in halos[:3]:
+        copy.wait()
+
+    inv_main = 1.0 / (1.0 + rpad[main])
+    inv_edge = 1.0 / (1.0 + rpad[edge])
+    along = fine_ratio * (2 * pos - 1).astype(f32)
+    ACROSS = ((-fine_ratio, ny - 1), (fine_ratio, 1))
+    MAIN = [(0, 0), (0, 1), (1, 0), (0, 2), (2, 0)]
+
+    def moved(table, h, p, q, rows, rows_up):
+        across, shift = ACROSS[h]
+        bx = table[h, PLACE[p, q + 1], rows]
+        by = table[h, PLACE[p + 1, q], rows]
+        return (
+            table[h, PLACE[p, q], rows]
+            + along * (table[h, PLACE[p, q + 1], rows_up] - bx)
+            + across * (pltpu.roll(by, shift, 1) - by)
+        )
+
+    first_star = {}
+    for h in range(2):
+        for p, q in ORDERS:
+            if p + q < 4:
+                star = moved(bsum, h, p, q, main, up)
+                if (p, q) in MAIN:
+                    first_star[p, q] = star + first_star[p, q] if h else star
+                hsum[h, PLACE[p, q], main] = star * inv_main
+        for p, q in MAIN:
+            hsum[h, PLACE[p, q + 1], edge] = moved(bsum, h, p, q + 1, edge, edge_up) * inv_edge
+    components(0, lambda p, q: first_star[p, q])
     scatter(0)
-    scatter(1)
-
-    rate = rpad[...]
-    inv_main = 1.0 / (1.0 + rpad[main])
-    inv_up = 1.0 / (1.0 + rpad[up])
-    inv_edge = 1.0 / (1.0 + rpad[edge])
+    again = {
+        order: moved(hsum, 0, *order, main, up) + moved(hsum, 1, *order, main, up) for order in MAIN
+    }
+    components(2, lambda p, q: again[p, q])
+    scatter(2)
+
+    halos[3].wait()
 
     @pl.loop(0, chunks)
     def _(c):
         vx, vy0, half, _j = chunk_of(first, c)
         shift = ny - 1 - (ny - 2) * half
         ca = fine_ratio * jnp.abs(vx)
-        zero = jnp.zeros((nx, ny), f32)
-        acc = [zero] * 3
         for jj in range(HALF):
             k = c * HALF + jj
-            vy = vy0 + jj * DVY
-            cb = fine_ratio * jnp.abs(vy)
+            cb = fine_ratio * jnp.abs(vy0 + jj * DVY)
             cc = 1.0 - ca - cb
-            g = spad[k, main] * inv_main
-            star = cc * g + (ca * spad[k, up]) * inv_up + cb * pltpu.roll(g, shift, 1)
-            ys = vy * star
-            acc = [acc[0] + star, acc[1] + ys, acc[2] + vy * ys]
-        add_moments(2, vx, *acc)
-
-    scatter(2)
+            g = fpad[k, main]
+            spad[k, main] = (cc * g + ca * fpad[k, up] + cb * pltpu.roll(g, shift, 1)) * inv_main
+            h = fpad[k, edge]
+            spad[k, edge] = (cc * h + ca * fpad[k, edge_up] + cb * pltpu.roll(h, shift, 1)) * inv_edge
+
+    gather(1)
     gather(0)
-    gather(1)
     gather(2)
 
     gathered(0)
@@ -285,10 +330,17 @@
     phys[2, wide] = -0.5 / temp
     phys[3, wide] = rs / temp * (rate / (1.0 + rate))
 
-    @pl.loop(1, 3 + nx // TILE)
+    first_row = lax.broadcasted_iota(jnp.int32, (TILE, ny), 0) == 0
+    for n in range(4):
+        phys[n, pl.ds(0, TILE)] = jnp.where(
+            first_row, phys[n, pl.ds(end, TILE)], phys[n, pl.ds(TILE, TILE)]
+        )
+
+    @pl.loop(0, 1 + nx // TILE)
     def _(t):
-        rows = pl.ds(pl.multiple_of(t * TILE, TILE), TILE)
-        ux, uy, scale, amp = [phys[n, rows] for n in range(4)]
+        rows = pl.ds(pl.multiple_of((t + 1) * TILE, TILE), TILE)
+        inner = pl.ds(pl.multiple_of(jnp.where(t == 0, 0, (t + 1) * TILE), TILE), TILE)
+        ux, uy, scale, amp = [phys[n, inner] for n in range(4)]
         zero = jnp.zeros_like(ux)
 
         def half_sums(speeds, drift, keep):
@@ -323,6 +375,8 @@
         store(12, fine_ratio, xs, yp[1:])
         store(16, -fine_ratio, xs, ym[1:])
 
+    for c in range(4):
+        flux[8 + c, pl.ds(end, TILE)] = flux[8 + c, pl.ds(TILE, TILE)]
     gathered(2)
     below, above = pl.ds(2 * TILE - 1, nx), pl.ds(2 * TILE + 1, nx)
     for c in range(4):
@@ -367,8 +421,8 @@
         xe = phys[3, edge] * jnp.exp(de * de * phys[2, edge])
         for jj in range(HALF):
             k = c * HALF + jj
-            fpad[k, main] = spad[k, main] * inv_main + xm * yt[j0 + jj, main]
-            fpad[k, edge] = spad[k, edge] * inv_edge + xe * yt[j0 + jj, edge]
+            fpad[k, main] = spad[k, main] + xm * yt[j0 + jj, main]
+            fpad[k, edge] = spad[k, edge] + xe * yt[j0 + jj, pl.ds(TILE, TILE)]
         for jj in range(HALF):
             k = c * HALF + jj
             cb = fine_ratio * jnp.abs(vy0 + jj * DVY)
@@ -379,9 +433,9 @@
     def _():
         for copy in onward(w):
             copy.wait_recv()
-        moved = coarse(vfull, vh)
+        stepped_on = coarse(vfull, vh)
         for c in range(4):
-            corr[c] = moved[c] + delta[c]
+            corr[c] = stepped_on[c] + delta[c]
         pass_on()
 
     corr_out[...] = corr[...]
@@ -479,6 +533,8 @@
             vmem((count, pad, ny), f32),
             vmem((count, pad, ny), f32),
             vmem((pad, ny), f32),
+            vmem((2, len(ORDERS), pad, ny), f32),
+            vmem((2, len(ORDERS), pad, ny), f32),
             vmem((3, 4, nx, ny), f32),
             vmem((3, nv - 1, band, ny), f32),
             vmem((3, 4, nx, ny), f32),
@@ -490,7 +546,7 @@
             vmem((20, pad, ny), f32),
             vmem((4, pad, ny), f32),
             vmem((4, nx, ny), f32),
-            dma((2,)), dma((3,)), dma((3,)), dma((3,)), dma((3,)), dma((3,)), dma((3,)),
+            dma((2,)), dma((4,)), dma((4,)), dma((3,)), dma((3,)), dma((3,)), dma((3,)),
             dma((4,)), dma((2,)), dma((3,)), dma((3,)),
         ],
         compiler_params=pltpu.CompilerParams(

time: 29 us -> 25.8 us (0.89)
  Pallas kernels: 28.2 us -> 25 us
    pallas_call x1, Pallas kernels: 25.5 us -> 22.3 us  [per_device(): pl.pallas_call(functools.partial(advance_kernel, nw, nv, owners), out_sha...]
where the time goes in v3:
time: 25.8 us; the launch traced here: 25.7 us
  Pallas kernels  25 us (97%)
  between operations  0.65 us (3%)
    pallas_call x1, Pallas kernels, per_device(): pl.pallas_call(functools.partial(advance_kernel, nw, nv, owners), out_sha...  22.3 us
    pallas_call x1, Pallas kernels, per_device(): pl.pallas_call(functools.partial(lift_kernel, parts), out_shape=(jax.Shap...  2.68 us

profile of v3, /device:TPU:0, one launch (start us, length us, event | category | flops | bytes accessed | tf_op | source)
XLA Modules:
  0.0 25.7 jit_solution(9062069473992333846)
XLA Ops:
  0.6 0.0 copy-start
  0.6 22.3 %advance.1 = (f32[192,32,128]{2,1,0:T(8,128)S(1)}, f32[4,32,128]{2,1,0:T(8,128)S(1)}, f32[4,32,128]{2,1,0:T(8,128)S(1)}) custom-call(f32[192,32,128]{2,1,0:T(8,128)} %bitcast.3, f32[32,128]{1,0:T(8,128)} %r.3), custom_call_target="tpu_custom_call" | custom-call | tf_op jit(solution)/shard_map/advance/pallas_call | solution.py:527
  23.0 0.0 copy-done
  23.0 2.7 %lift.1 = (f32[192,32,128]{2,1,0:T(8,128)}, f32[4,32,128]{2,1,0:T(8,128)}) custom-call(f32[192,32,128]{2,1,0:T(8,128)S(1)} %get-tuple-element.7.star2, f32[4,32,128]{2,1,0:T(8,128)S(1)} %get-tuple-element.8.corr, f32[4,32,128]{2,1,0:T(8,128)S(1)} %get-tuple-element.9.ending, f32[32,128]{1,0:T(8,128)S(1)} %copy-done), custom_call_target="tpu_custom_call" | custom-call | tf_op jit(solution)/shard_map/lift/pallas_call | solution.py:560
Async XLA Ops:
  0.6 22.4 %copy-start = (f32[32,128]{1,0:T(8,128)S(1)}, f32[32,128]{1,0:T(8,128)}, u32[]{:S(2)}) copy-start(f32[32,128]{1,0:T(8,128)} %r.3) | copy-start | bytes 49156

commit v4 on v3

--- a/solution.py
+++ b/solution.py
@@ -43,11 +43,18 @@
     return vx, vy, j // HALF, j
 
 
+def framed(main, above, below):
+    tile = (TILE, main.shape[1])
+    return jnp.concatenate(
+        [jnp.broadcast_to(above, tile), main, jnp.broadcast_to(below, tile)], axis=0
+    )
+
+
 def coarse(main, halo):
     nx = main.shape[1]
     rows = nx + 2 * TILE
-    u = [jnp.concatenate([halo[0, c], main[c], halo[1, c]], axis=0) for c in range(4)]
-    ny = u[0].shape[1]
+    ny = main.shape[2]
+    u = [framed(main[c], halo[0, c], halo[1, c]) for c in range(4)]
     rs, ux, uy, temp = physical_variables(u)
     p = rs * temp
     wave = jnp.sqrt(2.0 * temp)
@@ -74,8 +81,8 @@
 
 def advance_kernel(
     nw, nv, owners,
-    f, r, star2, corr_out, e_out,
-    fpad, spad, rpad, bsum, hsum, part, red_in, full, uh, vfull, vh, corr, yt, flux, phys, delta,
+    f, r, star2, corr_out,
+    fpad, spad, rpad, bsum, hsum, part, red_in, full, uh, edge_rows, vfull, vh, corr, corr_rows, e_out, ye, yt, flux, phys, delta,
     load_sem, halo_send, halo_recv, rs_send, rs_recv, ag_send, ag_recv, edge_send, edge_recv,
     win_send, win_recv,
 ):
@@ -165,12 +172,14 @@
                 ).start()
             if ph < 2:
                 row = (v * band) % nx
+                edge_rows[ph, 0] = total[:1]
+                edge_rows[ph, 1] = total[-1:]
 
                 @pl.when(row == 0)
                 def _():
                     for d in range(nv):
                         remote(
-                            full.at[ph, comp, pl.ds(0, TILE)], uh.at[ph, 1, comp],
+                            edge_rows.at[ph, 0], uh.at[ph, 1, comp],
                             edge_send.at[2 * ph], edge_recv.at[ph], (w, peer(d), other),
                         ).start()
 
@@ -178,7 +187,7 @@
                 def _():
                     for d in range(nv):
                         remote(
-                            full.at[ph, comp, pl.ds(nx - TILE, TILE)], uh.at[ph, 0, comp],
+                            edge_rows.at[ph, 1], uh.at[ph, 0, comp],
                             edge_send.at[2 * ph + 1], edge_recv.at[ph], (w, peer(d), other),
                         ).start()
 
@@ -320,9 +329,13 @@
     gather(0)
     gather(2)
 
+    gathered(1)
+    stepped = coarse(full.at[1], uh.at[1])
+    for c in range(4):
+        delta[c] = stepped[c]
     gathered(0)
     wide = pl.ds(TILE, nx + 2 * TILE)
-    u = [jnp.concatenate([uh[0, 0, c], full[0, c], uh[0, 1, c]], axis=0) for c in range(4)]
+    u = [framed(full[0, c], uh[0, 0, c], uh[0, 1, c]) for c in range(4)]
     rs, ux, uy, temp = physical_variables(u)
     rate = rpad[wide]
     phys[0, wide] = ux
@@ -386,17 +399,22 @@
             + flux[4 + c, below] + flux[8 + c, above]
             + pltpu.roll(to_y, 1, 1) + pltpu.roll(from_y, ny - 1, 1)
         )
-    gathered(1)
-    stepped = coarse(full.at[1], uh.at[1])
     for c in range(4):
-        delta[c] = e_out[c] - stepped[c]
+        start_step = delta[c]
+        delta[c] = e_out[c] - start_step
+        corr[c] = start_step
 
     def onward(n):
         return [
             remote(corr, vfull, win_send.at[0], win_recv.at[0], (n, v, s)),
-            remote(corr.at[:, pl.ds(0, TILE)], vh.at[1], win_send.at[1], win_recv.at[1], (n, v, other)),
-            remote(corr.at[:, pl.ds(nx - TILE, TILE)], vh.at[0], win_send.at[2], win_recv.at[2], (n, v, other)),
+            remote(corr_rows.at[0], vh.at[1], win_send.at[1], win_recv.at[1], (n, v, other)),
+            remote(corr_rows.at[1], vh.at[0], win_send.at[2], win_recv.at[2], (n, v, other)),
         ]
+
+    def store_corrected(c, value):
+        corr[c] = value
+        corr_rows[0, c] = value[:1]
+        corr_rows[1, c] = value[-1:]
 
     def pass_on():
         @pl.when(w + 1 < nw)
@@ -407,8 +425,17 @@
     @pl.when(w == 0)
     def _():
         for c in range(4):
-            corr[c] = stepped[c] + delta[c]
+            store_corrected(c, corr[c] + delta[c])
         pass_on()
+
+    rs, ux, uy, temp = physical_variables(e_out)
+    scale = -0.5 / temp
+    phys[4, main] = ux
+    phys[5, main] = scale
+    phys[6, main] = rs / temp * inv_main
+    for j in range(NVY):
+        d = (-vel_max + (j + 0.5) * DVY) - uy
+        ye[j] = jnp.exp(d * d * scale)
 
     @pl.loop(0, chunks)
     def _(c):
@@ -418,6 +445,8 @@
         dm = vx - phys[0, main]
         xm = phys[3, main] * jnp.exp(dm * dm * phys[2, main])
         de = vx - phys[0, edge]
+        dn = vx - phys[4, main]
+        x_end = phys[6, main] * jnp.exp(dn * dn * phys[5, main])
         xe = phys[3, edge] * jnp.exp(de * de * phys[2, edge])
         for jj in range(HALF):
             k = c * HALF + jj
@@ -427,7 +456,8 @@
             k = c * HALF + jj
             cb = fine_ratio * jnp.abs(vy0 + jj * DVY)
             g = fpad[k, main]
-            star2[k] = (1.0 - ca - cb) * g + ca * fpad[k, up] + cb * pltpu.roll(g, shift, 1)
+            star = (1.0 - ca - cb) * g + ca * fpad[k, up] + cb * pltpu.roll(g, shift, 1)
+            star2[k] = star * inv_main - x_end * ye[j0 + jj]
 
     @pl.when(w > 0)
     def _():
@@ -435,7 +465,7 @@
             copy.wait_recv()
         stepped_on = coarse(vfull, vh)
         for c in range(4):
-            corr[c] = stepped_on[c] + delta[c]
+            store_corrected(c, stepped_on[c] + delta[c])
         pass_on()
 
     corr_out[...] = corr[...]
@@ -472,22 +502,16 @@
     owner(edges)
 
 
-def lift_kernel(parts, star2, corr, ending, r, lifted, corrected, ye, yc, out, save_sem):
+def lift_kernel(parts, star2, corr, lifted, corrected, yc, out, save_sem):
     count = star2.shape[0]
     first = lax.axis_index("vel") * count
     corrected[...] = corr[...]
-    inv = 1.0 / (1.0 + r[...])
-    sides = []
-    for u, table in ((ending, ye), (corr, yc)):
-        rs, ux, uy, temp = physical_variables(u)
-        scale = -0.5 / temp
-        amp = rs / temp
-        sides.append((ux, scale, amp))
-        for j in range(NVY):
-            d = (-vel_max + (j + 0.5) * DVY) - uy
-            table[j] = jnp.exp(d * d * scale)
-    (ue, se, me), (uc, sc, mc) = sides
-    me = me * inv
+    rs, uc, uy, temp = physical_variables(corr)
+    sc = -0.5 / temp
+    mc = rs / temp
+    for j in range(NVY):
+        d = (-vel_max + (j + 0.5) * DVY) - uy
+        yc[j] = jnp.exp(d * d * sc)
     chunks = count // HALF
     per = chunks // parts
 
@@ -500,12 +524,11 @@
         @pl.loop(n * per, (n + 1) * per)
         def _(c):
             vx, _vy, _half, j0 = chunk_of(first, c)
-            de, dc = vx - ue, vx - uc
-            xe = me * jnp.exp(de * de * se)
+            dc = vx - uc
             xc = mc * jnp.exp(dc * dc * sc)
             for jj in range(HALF):
                 k = c * HALF + jj
-                out[k] = star2[k] * inv - xe * ye[j0 + jj] + xc * yc[j0 + jj]
+                out[k] = star2[k] + xc * yc[j0 + jj]
 
         save(n).start()
     for n in range(parts):
@@ -524,11 +547,11 @@
     in_vmem = pl.BlockSpec(memory_space=pltpu.VMEM)
     in_hbm = pl.BlockSpec(memory_space=pltpu.HBM)
     field = pltpu.with_memory_space_constraint(field, pltpu.HBM)
-    star2, corr, ending = pl.pallas_call(
+    star2, corr = pl.pallas_call(
         functools.partial(advance_kernel, nw, nv, owners),
-        out_shape=(jax.ShapeDtypeStruct((count, nx, ny), f32), small, small),
+        out_shape=(jax.ShapeDtypeStruct((count, nx, ny), f32), small),
         in_specs=[in_hbm, in_hbm],
-        out_specs=(in_vmem, in_vmem, in_vmem),
+        out_specs=(in_vmem, in_vmem),
         scratch_shapes=[
             vmem((count, pad, ny), f32),
             vmem((count, pad, ny), f32),
@@ -538,13 +561,17 @@
             vmem((3, 4, nx, ny), f32),
             vmem((3, nv - 1, band, ny), f32),
             vmem((3, 4, nx, ny), f32),
-            vmem((2, 2, 4, TILE, ny), f32),
+            vmem((2, 2, 4, 1, ny), f32),
+            vmem((2, 2, 1, ny), f32),
             vmem((4, nx, ny), f32),
-            vmem((2, 4, TILE, ny), f32),
+            vmem((2, 4, 1, ny), f32),
             vmem((4, nx, ny), f32),
+            vmem((2, 4, 1, ny), f32),
+            vmem((4, nx, ny), f32),
+            vmem((NVY, nx, ny), f32),
             vmem((NVY, pad, ny), f32),
             vmem((20, pad, ny), f32),
-            vmem((4, pad, ny), f32),
+            vmem((7, pad, ny), f32),
             vmem((4, nx, ny), f32),
             dma((2,)), dma((4,)), dma((4,)), dma((3,)), dma((3,)), dma((3,)), dma((3,)),
             dma((4,)), dma((2,)), dma((3,)), dma((3,)),
@@ -560,14 +587,14 @@
     lifted, corrected = pl.pallas_call(
         functools.partial(lift_kernel, parts),
         out_shape=(jax.ShapeDtypeStruct((count, nx, ny), f32), small),
-        in_specs=[in_vmem] * 4,
+        in_specs=[in_vmem] * 2,
         out_specs=(in_hbm, in_vmem),
         scratch_shapes=[
-            vmem((NVY, nx, ny), f32), vmem((NVY, nx, ny), f32), vmem((count, nx, ny), f32), dma((parts,)),
+            vmem((NVY, nx, ny), f32), vmem((count, nx, ny), f32), dma((parts,)),
         ],
         compiler_params=pltpu.CompilerParams(vmem_limit_bytes=16 << 20),
         name="lift",
-    )(star2, corr, ending, relax_rate)
+    )(star2, corr)
     return corrected[None], lifted[None]
 
 

time: 25.8 us -> 24.2 us (0.938)
  Pallas kernels: 25 us -> 23.4 us
    pallas_call x1, Pallas kernels: 22.3 us -> 20.9 us  [per_device(): pl.pallas_call(functools.partial(advance_kernel, nw, nv, owners), out_sha...]
where the time goes in v4:
time: 24.2 us; the launch traced here: 24.1 us
  Pallas kernels  23.4 us (97%)
  between operations  0.64 us (3%)
    pallas_call x1, Pallas kernels, per_device(): pl.pallas_call(functools.partial(advance_kernel, nw, nv, owners), out_sha...  20.9 us
    pallas_call x1, Pallas kernels, per_device(): pl.pallas_call(functools.partial(lift_kernel, parts), out_shape=(jax.Shap...  2.53 us

profile of v4, /device:TPU:0, one launch (start us, length us, event | category | flops | bytes accessed | tf_op | source)
XLA Modules:
  0.0 24.1 jit_solution(85277996790760867)
XLA Ops:
  0.6 20.9 %advance.1 = (f32[192,32,128]{2,1,0:T(8,128)S(1)}, f32[4,32,128]{2,1,0:T(8,128)S(1)}) custom-call(f32[192,32,128]{2,1,0:T(8,128)} %bitcast.3, f32[32,128]{1,0:T(8,128)} %r.1), custom_call_target="tpu_custom_call" | custom-call | tf_op jit(solution)/shard_map/advance/pallas_call | solution.py:550
  21.6 2.5 %lift.1 = (f32[192,32,128]{2,1,0:T(8,128)}, f32[4,32,128]{2,1,0:T(8,128)}) custom-call(f32[192,32,128]{2,1,0:T(8,128)S(1)} %get-tuple-element.6.star2, f32[4,32,128]{2,1,0:T(8,128)S(1)} %get-tuple-element.7.corr), custom_call_target="tpu_custom_call" | custom-call | tf_op jit(solution)/shard_map/lift/pallas_call | solution.py:587

commit v5 on v4

--- a/solution.py
+++ b/solution.py
@@ -103,9 +103,16 @@
     def peer(d):
         return lax.rem(v + d, nv)
 
-    load_f = pltpu.make_async_copy(f, fpad.at[:, main], load_sem.at[0])
-    load_r = pltpu.make_async_copy(r, rpad.at[main], load_sem.at[1])
-    load_f.start()
+    tiles = nx // TILE
+
+    def load_f(t):
+        rows = pl.ds(pl.multiple_of(t * TILE, TILE), TILE)
+        padded = pl.ds(pl.multiple_of((t + 2) * TILE, TILE), TILE)
+        return pltpu.make_async_copy(f.at[:, rows], fpad.at[:, padded], load_sem.at[t])
+
+    for t in range(tiles):
+        load_f(t).start()
+    load_r = pltpu.make_async_copy(r, rpad.at[main], load_sem.at[tiles])
     load_r.start()
 
     barrier = pltpu.get_barrier_semaphore()
@@ -210,12 +217,12 @@
         if ph < 2:
             settle(uh.at[ph], edge_recv.at[ph])
 
-    load_f.wait()
     parity = (first // HALF) % 2
     rounds = (chunks + 1) // 2
 
     @pl.loop(0, nx // TILE)
     def _(t):
+        load_f(t).wait()
         rows = pl.ds(pl.multiple_of(2 * TILE + t * TILE, TILE), TILE)
         for h in range(2):
             acc = {order: jnp.zeros((TILE, ny), f32) for order in ORDERS}
@@ -357,17 +364,29 @@
         zero = jnp.zeros_like(ux)
 
         def half_sums(speeds, drift, keep):
-            sums = {0: [zero] * 4, 1: [zero] * 4}
+            weights = []
             for n, speed in enumerate(speeds):
                 d = speed - drift
                 e = jnp.exp(d * d * scale)
                 if keep:
                     yt[n, rows] = e
-                side = sums[int(speed > 0)]
-                e1 = speed * e
-                e2 = speed * e1
-                sums[int(speed > 0)] = [side[0] + e, side[1] + e1, side[2] + e2, side[3] + speed * e2]
-            return sums[1], sums[0]
+                weights.append(e)
+            sides = []
+            half = len(speeds) // 2
+            for at, c in ((half, 0.5 * vel_max), (0, -0.5 * vel_max)):
+                m = [zero] * 4
+                for n in range(half // 2, half):
+                    t = speeds[at + n] - c
+                    high, low = weights[at + n], weights[at + half - 1 - n]
+                    even, odd = high + low, high - low
+                    m = [m[0] + even, m[1] + t * odd, m[2] + t**2 * even, m[3] + t**3 * odd]
+                sides.append([
+                    m[0],
+                    m[1] + c * m[0],
+                    m[2] + (2 * c) * m[1] + c**2 * m[0],
+                    m[3] + (3 * c) * m[2] + (3 * c**2) * m[1] + c**3 * m[0],
+                ])
+            return sides
 
         xp, xm = half_sums([-vel_max + (i + 0.5) * DVX for i in range(NVX)], ux, False)
         yp, ym = half_sums([-vel_max + (j + 0.5) * DVY for j in range(NVY)], uy, True)
@@ -573,7 +592,7 @@
             vmem((20, pad, ny), f32),
             vmem((7, pad, ny), f32),
             vmem((4, nx, ny), f32),
-            dma((2,)), dma((4,)), dma((4,)), dma((3,)), dma((3,)), dma((3,)), dma((3,)),
+            dma((1 + nx // TILE,)), dma((4,)), dma((4,)), dma((3,)), dma((3,)), dma((3,)), dma((3,)),
             dma((4,)), dma((2,)), dma((3,)), dma((3,)),
         ],
         compiler_params=pltpu.CompilerParams(

time: 24.2 us -> 23.8 us (0.983)
  Pallas kernels: 23.4 us -> 23 us
    pallas_call x1, Pallas kernels: 20.9 us -> 20.4 us  [per_device(): pl.pallas_call(functools.partial(advance_kernel, nw, nv, owners), out_sha...]
where the time goes in v5:
time: 23.8 us; the launch traced here: 23.6 us
  Pallas kernels  23 us (97%)
  between operations  0.64 us (3%)
    pallas_call x1, Pallas kernels, per_device(): pl.pallas_call(functools.partial(advance_kernel, nw, nv, owners), out_sha...  20.4 us
    pallas_call x1, Pallas kernels, per_device(): pl.pallas_call(functools.partial(lift_kernel, parts), out_shape=(jax.Shap...  2.53 us

profile of v5, /device:TPU:0, one launch (start us, length us, event | category | flops | bytes accessed | tf_op | source)
XLA Modules:
  0.0 23.6 jit_solution(9566149890516334790)
XLA Ops:
  0.6 20.4 %advance.1 = (f32[192,32,128]{2,1,0:T(8,128)S(1)}, f32[4,32,128]{2,1,0:T(8,128)S(1)}) custom-call(f32[192,32,128]{2,1,0:T(8,128)} %bitcast.3, f32[32,128]{1,0:T(8,128)} %r.1), custom_call_target="tpu_custom_call" | custom-call | tf_op jit(solution)/shard_map/advance/pallas_call | solution.py:569
  21.1 2.5 %lift.1 = (f32[192,32,128]{2,1,0:T(8,128)}, f32[4,32,128]{2,1,0:T(8,128)}) custom-call(f32[192,32,128]{2,1,0:T(8,128)S(1)} %get-tuple-element.6.star2, f32[4,32,128]{2,1,0:T(8,128)S(1)} %get-tuple-element.7.corr), custom_call_target="tpu_custom_call" | custom-call | tf_op jit(solution)/shard_map/lift/pallas_call | solution.py:606
